TPU v7x, 128 devices: a whole 4x4x4 slice. The times are simulated.
128 devices in a mesh: section: 8 (over y, core), expert: 16 (over x, z).
Axes of the slice: x: 4, y: 4, z: 4, core: 2. Of those that a mesh axis runs over, the one named last changes fastest.
Arguments:
- section_input: bfloat16 [8, 2048, 2880], P('section', 'expert'), may hold values from -6 to 6
- attention_gain: float32 [8, 2880], P('section'), may hold values from 0.1 to 1.9
- query_key_value_weight: bfloat16 [8, 2880, 2560], P('section', 'expert'), may hold values from -0.109375 to 0.109375
- qkv_bias: float32 [8, 2560], P('section'), may hold values from -3 to 8
- out_weight: bfloat16 [8, 2048, 2880], P('section'), may hold values from -0.125 to 0.125
- out_bias: float32 [8, 2880], P('section'), may hold values from -3 to 3
- attention_sink_logits: float32 [8, 32], P('section'), may hold values from -1 to 250
- expert_gain: float32 [8, 2880], P('section'), may hold values from 0.1 to 1.9
- gate_up_weight: bfloat16 [8, 16, 2880, 1440], P('section', 'expert'), may hold values from -0.109375 to 0.109375
- down_weight: bfloat16 [8, 16, 720, 2880], P('section', 'expert'), may hold values from -0.15625 to 0.15625
- expert_ids: int32 [8, 2048, 4], P('section', 'expert'), may hold values from 0 to 7, all different within a row; in each aligned block of 128 rows (0 to 127, 128 to 255, ..., all dimensions but the last counted through in order) at most 80 rows name the same one
- gate_logits: float32 [8, 2048, 4], P('section', 'expert'), may hold values from -8 to 204
- placement: int32 [8, 8], P('section'), may hold values from 0 to 7, each once within a row
Outputs:
- section_output: bfloat16 [8, 2048, 2880], P('section', 'expert')
Inputs may be any that keep to these rules, and one draw needn't show every extreme that they name: `expert_ids`: within each section, among the 128 tokens of one device no expert is named more than 80 times, a bound that some block reaches. `placement`: each row names every expert once.
All inputs are finite; a program needn't handle non-finite values.
Results may differ from a plain program's by a relative error of at most 0.018.
Values may be sent and summed in bfloat16 or wider, within the bound.
A program may use at most 128 MiB of HBM per device.

v0:
```python
import jax
import jax.numpy as jnp
from jax import lax
from jax.sharding import PartitionSpec as P

HEAD_DIM = 64
QUERY_HEADS = 32
KEY_VALUE_HEADS = 4
WINDOW_TOKENS = 128
TOP = 4


def from_behind(x, axis, by):
    size = lax.axis_size(axis)
    pairs = [(i, i + by) for i in range(size) if 0 <= i + by < size]
    return lax.ppermute(x, axis, pairs)


def passed_along(x, axis, by):
    size = lax.axis_size(axis)
    return lax.ppermute(x, axis, [(i, (i + by) % size) for i in range(size)])


def normed(vector, gain_row):
    as_float = vector.astype(jnp.float32)
    inverse_rms = lax.rsqrt(jnp.mean(as_float * as_float, axis=-1, keepdims=True) + 1e-05)
    return (as_float * inverse_rms * gain_row).astype(jnp.bfloat16)


def swiglu(hidden):
    half_cols = hidden.shape[1] // 2
    gate_part = hidden[:, :half_cols]
    up_part = hidden[:, half_cols:]
    return ((up_part + 1.0) * gate_part * jax.nn.sigmoid(1.702 * gate_part)).astype(jnp.bfloat16)


def shards(
    section_input,
    attention_gain,
    query_key_value_weight,
    qkv_bias,
    out_weight,
    out_bias,
    attention_sink_logits,
    expert_gain,
    gate_up_weight,
    down_weight,
    expert_ids,
    gate_logits,
    placement,
):
    count_of_rows = section_input.shape[1]
    model_width = section_input.shape[2]
    experts_count = placement.shape[1]
    slot_count = 2 * min(count_of_rows // 2, count_of_rows * TOP * 5 // (8 * experts_count))
    offset = lax.axis_index("expert") * count_of_rows
    query_group_width = QUERY_HEADS // KEY_VALUE_HEADS
    tile_gu = gate_up_weight[0, 0]
    tile_down = down_weight[0, 0]
    state = section_input[0]
    normed_in = normed(state, attention_gain[0])
    projected_rows = (
        jnp.dot(
            normed_in,
            lax.all_gather(query_key_value_weight[0], "expert", axis=0, tiled=True),
            preferred_element_type=jnp.float32,
        )
        + qkv_bias[0]
    ).astype(jnp.bfloat16)
    query_rows = projected_rows[:, : QUERY_HEADS * HEAD_DIM].reshape(
        count_of_rows, KEY_VALUE_HEADS, query_group_width, HEAD_DIM
    )
    key_value = projected_rows[:, QUERY_HEADS * HEAD_DIM :]
    rim_rows = from_behind(key_value, "expert", 1)
    rows_in_window = jnp.concatenate([rim_rows, key_value], 0)
    key_row_slice = rows_in_window[:, : KEY_VALUE_HEADS * HEAD_DIM].reshape(
        WINDOW_TOKENS + count_of_rows, KEY_VALUE_HEADS, HEAD_DIM
    )
    value_row_slice = rows_in_window[:, KEY_VALUE_HEADS * HEAD_DIM :].reshape(
        WINDOW_TOKENS + count_of_rows, KEY_VALUE_HEADS, HEAD_DIM
    )
    scores = (
        jnp.einsum("ikgd,jkd->kgij", query_rows, key_row_slice, preferred_element_type=jnp.float32)
        * 0.125
    )
    query_pos = offset + jnp.arange(count_of_rows, dtype=jnp.int32)
    key_pos = offset - WINDOW_TOKENS + jnp.arange(WINDOW_TOKENS + count_of_rows, dtype=jnp.int32)
    distance = query_pos[:, None] - key_pos[None, :]
    inside = (distance >= 0) & (distance < WINDOW_TOKENS) & (key_pos >= 0)[None, :]
    head_sink_logit = attention_sink_logits[0].reshape(KEY_VALUE_HEADS, query_group_width)[
        :, :, None
    ]
    masked = jnp.where(inside, scores, -1e30)
    peak = jnp.maximum(jnp.max(masked, axis=-1), head_sink_logit)
    numer = jnp.where(inside, jnp.exp(masked - peak[..., None]), 0.0)
    denominator = jnp.sum(numer, axis=-1) + jnp.exp(head_sink_logit - peak)
    attention = (numer / denominator[..., None]).astype(jnp.bfloat16)
    mixed = jnp.einsum(
        "kgij,jkd->ikgd", attention, value_row_slice, preferred_element_type=jnp.float32
    )
    attended = mixed.astype(jnp.bfloat16).reshape(count_of_rows, QUERY_HEADS * HEAD_DIM)
    residual = (
        state.astype(jnp.float32)
        + jnp.dot(attended, out_weight[0], preferred_element_type=jnp.float32)
        + out_bias[0]
    ).astype(jnp.bfloat16)
    normed_mid = normed(residual, expert_gain[0])
    flat_ids = expert_ids[0].reshape(-1)
    expert_range = jnp.arange(experts_count, dtype=jnp.int32)
    one_hot = (flat_ids[:, None] == expert_range[None, :]).astype(jnp.int32)
    slot_of = jnp.sum((jnp.cumsum(one_hot, axis=0) - 1) * one_hot, axis=-1)
    token_of = jnp.arange(count_of_rows * TOP, dtype=jnp.int32) // TOP
    source_rows = (
        jnp.full((experts_count * slot_count,), -1, jnp.int32)
        .at[flat_ids * slot_count + slot_of]
        .set(token_of)
    )
    valid_rows = (source_rows >= 0)[:, None].astype(jnp.bfloat16)
    gathered = jnp.take(normed_mid, jnp.maximum(source_rows, 0), axis=0) * valid_rows
    by_expert = gathered.reshape(experts_count, slot_count, model_width)
    holders = placement[0]
    by_pair = jnp.take(by_expert, holders, axis=0)
    matches = (holders[:, None] == expert_range[None, :]).astype(jnp.int32)
    holder_of = jnp.sum(expert_range[:, None] * matches, axis=0)
    outgoing = jnp.repeat(by_pair, 2, axis=0)
    rows_in = lax.all_to_all(outgoing, "expert", split_axis=0, concat_axis=0, tiled=True)
    in_shape = rows_in.shape
    hidden = jnp.dot(rows_in.reshape(-1, model_width), tile_gu, preferred_element_type=jnp.float32)
    returned = lax.all_to_all(
        jnp.dot(swiglu(hidden), tile_down, preferred_element_type=jnp.float32)
        .astype(jnp.bfloat16)
        .reshape(in_shape),
        "expert",
        split_axis=0,
        concat_axis=0,
        tiled=True,
    )
    paired = returned.astype(jnp.float32).reshape(experts_count, 2, slot_count, model_width)
    summed = (
        (paired[:, 0] + paired[:, 1])
        .astype(jnp.bfloat16)
        .reshape(experts_count * slot_count, model_width)
    )
    picked = jnp.take(summed, holder_of[flat_ids] * slot_count + slot_of, axis=0).reshape(
        count_of_rows, TOP, model_width
    )
    picked = lax.optimization_barrier(picked).astype(jnp.float32)
    gate_weights = jax.nn.softmax(gate_logits[0], axis=-1)
    fresh = (
        residual.astype(jnp.float32) + jnp.sum(picked * gate_weights[..., None], axis=1)
    ).astype(jnp.bfloat16)
    moved = passed_along(fresh, "section", 1)
    return moved[None]


def solution(mesh):
    return jax.shard_map(
        shards,
        mesh=mesh,
        in_specs=(
            P("section", "expert", None),
            P("section", None),
            P("section", "expert", None),
            P("section", None),
            P("section", None, None),
            P("section", None),
            P("section", None),
            P("section", None),
            P("section", "expert", None, None),
            P("section", "expert", None, None),
            P("section", "expert", None),
            P("section", "expert", None),
            P("section", None),
        ),
        out_specs=P("section", "expert", None),
        check_vma=False,
    )
```

profile of v0, /device:TPU:0, one launch (start us, length us, event | category | flops | bytes accessed | tf_op | source)
XLA Modules:
  0.0 547.5 jit_solution(6834803989660928297)
XLA Ops:
  6.6 4.0 copy.62
  13.5 4.4 compare_select_fusion.4
  18.5 2.4 scatter_custom_fusion
  21.6 168.0 %all-gather.3.cloned.1.call-done = bf16[1,2880,2560]{2,0,1:T(2,128)(2,1)} async-done(((bf16[1,180,2560]{2,0,1:T(2,128)(2,1)}), bf16[1,2880,2560]{2,0,1:T(2,128)(2,1)}) %all-gather.3.cloned.1.call-update) | async-done | bytes 14745616 | tf_op jit(solution)/shard_map/all_gather | solution.py:65
  189.7 15.2 %fusion.17 = bf16[128,2560]{1,0:T(8,128)(2,1)S(1)} fusion(bf16[1,2880,2560]{2,0,1:T(2,128)(2,1)} %all-gather.3.cloned.1.call-done, bf16[1,128,2880]{1,2,0:T(8,128)(2,1)S(1)} %copy-done.2, f32[2880]{0:T(1024)S(1)} %reduce.1, f32[128]{0:T(128)S(1)} %add_rsqrt_fusion.1, f32[2560]{0:T(1024)S(1)} %reduce.2), kind=kOutput, calls=%fused_computation.29 | convolution fusion | flops 1889566720 | bytes 16160512 | tf_op jit(solution)/shard_map/dot_general | solution.py:63
  204.9 3.7 collective-permute-start
  216.6 3.3 multiply_reduce_fusion.1
  221.8 4.6 gather_fusion
  226.4 4.5 select_multiply_fusion
  230.9 4.9 gather_fusion.1
  235.7 2.5 broadcast_select_fusion
  238.8 93.2 %all_to_all.10 = bf16[16,80,2880]{2,1,0:T(8,128)(2,1)S(1)} all-to-all(bf16[16,80,2880]{2,1,0:T(8,128)(2,1)S(1)} %bitcast.119), channel_id=1, replica_groups=mesh['section'=8,'expert'=16] {'expert'}, dimensions={0} | all-to-all | bytes 14745600 | tf_op jit(solution)/shard_map/all_to_all | solution.py:126
  332.0 15.5 %fusion.5 = f32[1280,1440]{0,1:T(8,128)} fusion(bf16[1280,2880]{1,0:T(8,128)(2,1)S(1)} %bitcast.121, bf16[1,1,2880,1440]{2,3,1,0:T(8,128)(2,1)} %param.21), kind=kOutput, calls=%fused_computation.10 | convolution fusion | flops 10616832000 | bytes 23040000 | tf_op jit(solution)/shard_map/dot_general | solution.py:128
  347.4 11.9 %convolution_convert_fusion = bf16[1280,2880]{0,1:T(8,128)(2,1)} fusion(bf16[1,1,720,2880]{3,2,1,0:T(8,128)(2,1)S(1)} %bitcast.134, f32[1280,1440]{0,1:T(8,128)} %fusion.5), kind=kOutput, calls=%fused_computation.9 | convolution fusion | flops 5319475200 | bytes 18892800 | tf_op jit(solution)/shard_map/dot_general | solution.py:130
  359.4 10.4 %copy.71 = bf16[1280,2880]{1,0:T(8,128)(2,1)} copy(bf16[1280,2880]{0,1:T(8,128)(2,1)} %convolution_convert_fusion) | data formatting | bytes 14745600 | tf_op jit(solution)/shard_map/convert_element_type | solution.py:131
  369.8 4.8 all-to-all-start.1
  375.0 112.0 %all-to-all-done.1 = bf16[16,80,2880]{2,1,0:T(8,128)(2,1)} async-done(((bf16[16,80,2880]{2,1,0:T(8,128)(2,1)}), bf16[16,80,2880]{2,1,0:T(8,128)(2,1)}, u32[]{:S(2)}, u32[]{:S(2)}) %all-to-all-start.1) | async-done | bytes 7372832 | tf_op jit(solution)/shard_map/all_to_all | solution.py:129
  487.0 9.5 %convert.4 = f32[8,2,80,2880]{3,2,1,0:T(8,128)} convert(bf16[8,2,80,2880]{3,2,1,0:T(8,128)(2,1)} %bitcast.36) | non-fusion elementwise | flops 3686400 | bytes 22118400 | tf_op jit(solution)/shard_map/reshape | solution.py:138
  496.5 7.8 %fusion.8 = bf16[8,1,80,2880]{3,2,0,1:T(8,128)(2,1)} fusion(f32[8,2,80,2880]{3,2,1,0:T(8,128)} %convert.4), kind=kLoop, calls=%fused_computation.14 | loop fusion | flops 3686400 | bytes 18432000 | tf_op jit(solution)/shard_map/convert_element_type | solution.py:141
  504.3 9.3 %gather_fusion.2 = bf16[512,2880]{1,0:T(8,128)(2,1)} fusion(bf16[640,2880]{1,0:T(8,128)(2,1)} %bitcast.117, s32[1024]{0:T(1024)S(1)} %pad_clamp_fusion), kind=kCustom, calls=%fused_computation.2 | custom fusion | bytes 5900288 | tf_op jit(solution)/shard_map/jit(_take)/gather | solution.py:144
  513.6 4.9 gather.24
  519.9 4.5 multiply_reduce_fusion
  524.4 1.6 copy.75
  527.5 12.1 %collective-permute-done.1 = bf16[128,2880]{0,1:T(8,128)(2,1)S(1)} collective-permute-done((bf16[128,2880]{0,1:T(8,128)(2,1)S(1)}, bf16[128,2880]{0,1:T(8,128)(2,1)S(1)}, u32[]{:S(2)}, u32[]{:S(2)}) %collective-permute-start.1) | collective-permute-done | bytes 737312 | tf_op jit(solution)/shard_map/ppermute | solution.py:21
  (100 shorter events, 18.6 us)
Async XLA Ops:
  6.5 4.0 copy-start.8
  6.5 4.5 copy-start.4
  6.5 4.5 copy-start.7
  6.5 6.0 %copy-start.9 = (s32[1,8]{1,0:T(1,128)S(1)}, s32[1,8]{1,0:T(1,128)}, u32[]{:S(2)}) copy-start(s32[1,8]{1,0:T(1,128)} %param.25) | copy-start | bytes 100
  6.5 14.5 %copy-start.2 = (bf16[1,128,2880]{1,2,0:T(8,128)(2,1)S(1)}, bf16[1,128,2880]{1,2,0:T(8,128)(2,1)}, u32[]{:S(2)}) copy-start(bf16[1,128,2880]{1,2,0:T(8,128)(2,1)} %param.13) | copy-start | bytes 2211844
  6.5 183.1 %all-gather.3.cloned.1.call-start = ((), (), s32[]{:S(2)}) async-start(), calls=%async_computation.2 | async-start | bytes 31334400 | tf_op jit(solution)/shard_map/all_gather | solution.py:65
  21.6 187.0 %copy-start.5 = (f32[1,2880]{1,0:T(1,128)S(1)}, f32[1,2880]{1,0:T(1,128)}, u32[]{:S(2)}) copy-start(f32[1,2880]{1,0:T(1,128)} %param.18) | copy-start | bytes 34564
  21.6 187.6 %copy-start.10 = (f32[1,32]{1,0:T(1,128)S(1)}, f32[1,32]{1,0:T(1,128)}, u32[]{:S(2)}) copy-start(f32[1,32]{1,0:T(1,128)} %param.19) | copy-start | bytes 388
  21.6 188.3 %copy-start.6 = (f32[1,2880]{1,0:T(1,128)S(1)}, f32[1,2880]{1,0:T(1,128)}, u32[]{:S(2)}) copy-start(f32[1,2880]{1,0:T(1,128)} %param.20) | copy-start | bytes 34564
  204.9 6.0 %collective-permute-start = (bf16[128,512]{1,0:T(8,128)(2,1)S(1)}, bf16[128,512]{1,0:T(8,128)(2,1)S(1)}, u32[]{:S(2)}, u32[]{:S(2)}) collective-permute-start(bf16[128,512]{1,0:T(8,128)(2,1)S(1)} %slice.55), channel_id=1, source_target_pairs={{0,1},{1,2},{2,3},{3,4},{4,5},{5,6},{6,7},{7,8},{8,9},{9,10},{10,1... | collective-permute-start | bytes 393224 | tf_op jit(solution)/shard_map/ppermute | solution.py:16
  211.9 2.5 slice-start
  213.1 2.5 slice-start.1
  213.1 3.5 slice-start.2
  219.9 1.2 copy-start
  238.8 108.7 %slice-start.3 = ((s8[4239360]{0:T(1024)(128)(4,1)}), s8[45056]{0:T(1024)(128)(4,1)S(1)}, s32[]{:S(2)}) async-start(s8[4239360]{0:T(1024)(128)(4,1)} %bitcast.133), calls=%async_computation.6 | async-start | bytes 90112
  332.0 15.5 %slice-start.4 = ((s8[4239360]{0:T(1024)(128)(4,1)}), s8[4194304]{0:T(1024)(128)(4,1)S(1)}, s32[]{:S(2)}) async-start(s8[4239360]{0:T(1024)(128)(4,1)} %bitcast.133), calls=%async_computation.7 | async-start | bytes 8388608
  369.8 5.0 copy-start.3
  369.8 117.2 %all-to-all-start.1 = ((bf16[16,80,2880]{2,1,0:T(8,128)(2,1)}), bf16[16,80,2880]{2,1,0:T(8,128)(2,1)}, u32[]{:S(2)}, u32[]{:S(2)}) async-start(bf16[16,80,2880]{2,1,0:T(8,128)(2,1)} %bitcast.118), calls=%async_computation.1 | async-start | bytes 15073280 | tf_op jit(solution)/shard_map/all_to_all | solution.py:129
  519.9 6.1 %copy-start.1 = (f32[128,2880]{0,1:T(8,128)S(1)}, f32[128,2880]{0,1:T(8,128)}, u32[]{:S(2)}) copy-start(f32[128,2880]{0,1:T(8,128)} %copy-done) | copy-start | bytes 4423684
  527.5 12.1 %collective-permute-start.1 = (bf16[128,2880]{0,1:T(8,128)(2,1)S(1)}, bf16[128,2880]{0,1:T(8,128)(2,1)S(1)}, u32[]{:S(2)}, u32[]{:S(2)}) collective-permute-start(bf16[128,2880]{0,1:T(8,128)(2,1)S(1)} %add_convert_fusion), channel_id=1, source_target_pairs={{0,16},{16,32},{32,48},{48,64},{64,80},{80,96},{96,112},{112,0},{1... | collective-permute-start | bytes 2211848 | tf_op jit(solution)/shard_map/ppermute | solution.py:21
Sparse Core Ops, SparseCore 0:
  10.7 178.9 all-gather.2
where the time goes:
time: 555 us; the launch traced here: 548 us
  waiting for transfers between devices  293 us (53%)
  blocking collectives  93.2 us (17%)
  local copies, waits for them, and re-layouts  50 us (9%)
  matrix products  47.9 us (9%)
  other arithmetic  41.3 us (7%)
  between operations  14.1 us (3%)
  starting transfers between devices  8.6 us (2%)
    all_gather x1, waiting for transfers between devices, shards(): lax.all_gather(query_key_value_weight[0], 'expert', axis=0, tiled=True)  168 us
    all_to_all x1, waiting for transfers between devices, shards(): lax.all_to_all(jnp.dot(swiglu(hidden), tile_down, preferred_element_type=...  112 us
    all_to_all x1, blocking collectives, shards(): lax.all_to_all(outgoing, 'expert', split_axis=0, concat_axis=0, tiled=True)  93.2 us
    dot_general x1, matrix products, shards(): jnp.dot(rows_in.reshape(-1, model_width), tile_gu, preferred_element_type...  15.5 us
    dot_general x1, matrix products, shards(): jnp.dot(normed_in, lax.all_gather(query_key_value_weight[0], 'expert', ax...  15.2 us
    gather x2, local copies, waits for them, and re-layouts, shards(): jnp.take(summed, holder_of[flat_ids] * slot_count + slot_of, axis=0)  14.1 us
    ppermute x1, waiting for transfers between devices, passed_along(): return lax.ppermute(x, axis, [(i, (i + by) % size) for i in range(size)])  12.1 us
    dot_general x1, matrix products, shards(): jnp.dot(swiglu(hidden), tile_down, preferred_element_type=jnp.float32)  11.9 us
  transfers between devices with their start and end apart: 4, of which 4 were waited for; matrix products, arithmetic and copies ran while one was open for 2% of the time, Pallas kernels for 0%

commit v1 on v0

--- a/solution.py
+++ b/solution.py
@@ -59,10 +59,19 @@
     tile_down = down_weight[0, 0]
     state = section_input[0]
     normed_in = normed(state, attention_gain[0])
+    meshes_push = lambda mesh_name, v0: jnp.concatenate(
+        lax.all_to_all(
+            jnp.stack(lax.axis_size(mesh_name) * [v0], axis=0),
+            axis_name=mesh_name,
+            split_axis=0,
+            concat_axis=0,
+        ),
+        axis=0,
+    )
     projected_rows = (
         jnp.dot(
             normed_in,
-            lax.all_gather(query_key_value_weight[0], "expert", axis=0, tiled=True),
+            meshes_push("expert", query_key_value_weight[0]),
             preferred_element_type=jnp.float32,
         )
         + qkv_bias[0]

time: 555 us -> 616 us (1.11); the launches traced: 548 us -> 615 us
  waiting for transfers between devices: 293 us -> 353 us
  local copies, waits for them, and re-layouts: 50 us -> 66.1 us
  between operations: 14.1 us -> 0.45 us
  starting transfers between devices: 8.6 us -> 21.5 us
  matrix products: 47.9 us -> 40.3 us
    all_to_all x0 -> x1, waiting for transfers between devices: none -> 249 us  [shards(): lax.all_to_all(jnp.stack(lax.axis_size(mesh_name) * [v0], axis=0), axis_n...]
    all_gather x1 -> x0, waiting for transfers between devices: 168 us -> none  [shards(): lax.all_gather(query_key_value_weight[0], 'expert', axis=0, tiled=True)]
    all_to_all x1, waiting for transfers between devices: 112 us -> 91.4 us  [shards(): lax.all_to_all(jnp.dot(swiglu(hidden), tile_down, preferred_element_type=...]
    reshape x0 -> x1, local copies, waits for them, and re-layouts: none -> 13.5 us  [shards(): jnp.concatenate(lax.all_to_all(jnp.stack(lax.axis_size(mesh_name) * [v0],...]
    all_to_all x0 -> x1, starting transfers between devices: none -> 8.15 us  [shards(): lax.all_to_all(jnp.stack(lax.axis_size(mesh_name) * [v0], axis=0), axis_n...]
    dot_general x1, matrix products: 15.2 us -> 7.53 us  [shards(): jnp.dot(normed_in, meshes_push('expert', query_key_value_weight[0]), pref...]
    another operation x1 -> x2, local copies, waits for them, and re-layouts: 0.01 us -> 6.56 us  [the longest x1 6.56 us: shards(): jnp.stack(lax.axis_size(mesh_name) * [v0], axis=0)]
where the time goes in v1:
time: 616 us; the launch traced here: 615 us
  waiting for transfers between devices  353 us (57%)
  blocking collectives  92.7 us (15%)
  local copies, waits for them, and re-layouts  66.1 us (11%)
  other arithmetic  41.3 us (7%)
  matrix products  40.3 us (7%)
  starting transfers between devices  21.5 us (3%)
    all_to_all x1, waiting for transfers between devices, shards(): lax.all_to_all(jnp.stack(lax.axis_size(mesh_name) * [v0], axis=0), axis_n...  249 us
    all_to_all x1, blocking collectives, shards(): lax.all_to_all(outgoing, 'expert', split_axis=0, concat_axis=0, tiled=True)  92.7 us
    all_to_all x1, waiting for transfers between devices, shards(): lax.all_to_all(jnp.dot(swiglu(hidden), tile_down, preferred_element_type=...  91.4 us
    dot_general x1, matrix products, shards(): jnp.dot(rows_in.reshape(-1, model_width), tile_gu, preferred_element_type...  15.5 us
    gather x2, local copies, waits for them, and re-layouts, shards(): jnp.take(summed, holder_of[flat_ids] * slot_count + slot_of, axis=0)  14.2 us
    reshape x1, local copies, waits for them, and re-layouts, shards(): jnp.concatenate(lax.all_to_all(jnp.stack(lax.axis_size(mesh_name) * [v0],...  13.5 us
  transfers between devices with their start and end apart: 4, of which 4 were waited for; matrix products, arithmetic and copies ran while one was open for 2% of the time, Pallas kernels for 0%

profile of v1, /device:TPU:0, one launch (start us, length us, event | category | flops | bytes accessed | tf_op | source)
XLA Modules:
  0.0 615.0 jit_solution(14002907000038139193)
XLA Ops:
  0.0 6.6 %stack.3 = bf16[16,180,2560]{2,1,0:T(8,128)(2,1)} broadcast(bf16[180,2560]{1,0:T(8,128)(2,1)} %bitcast.121), dimensions={1,2} | broadcast | bytes 15667200 | tf_op jit(solution)/shard_map/stack | solution.py:64
  6.6 8.1 %all-to-all-start = ((bf16[16,180,2560]{2,1,0:T(8,128)(2,1)}), bf16[16,180,2560]{2,1,0:T(8,128)(2,1)}, u32[]{:S(2)}, u32[]{:S(2)}) async-start(bf16[16,180,2560]{2,1,0:T(8,128)(2,1)} %stack.3), calls=%async_computation | async-start | bytes 30146560 | tf_op jit(solution)/shard_map/all_to_all | solution.py:63
  17.6 4.3 compare_select_fusion.4
  25.7 248.9 %all-to-all-done = bf16[16,180,2560]{2,1,0:T(8,128)(2,1)} async-done(((bf16[16,180,2560]{2,1,0:T(8,128)(2,1)}), bf16[16,180,2560]{2,1,0:T(8,128)(2,1)}, u32[]{:S(2)}, u32[]{:S(2)}) %all-to-all-start) | async-done | bytes 14745632 | tf_op jit(solution)/shard_map/all_to_all | solution.py:63
  274.6 13.5 %reshape.297 = bf16[2880,2560]{1,0:T(8,128)(2,1)} reshape(bf16[16,180,2560]{2,1,0:T(8,128)(2,1)} %all-to-all-done) | data formatting | bytes 29491200 | tf_op jit(solution)/shard_map/reshape | solution.py:62
  288.1 7.5 %fusion.11 = bf16[128,2560]{1,0:T(8,128)(2,1)S(1)} fusion(bf16[2880,2560]{1,0:T(8,128)(2,1)} %reshape.297, bf16[1,128,2880]{1,2,0:T(8,128)(2,1)S(1)} %copy-done.2, f32[2880]{0:T(1024)S(1)} %reduce.1, f32[128]{0:T(128)S(1)} %add_rsqrt_fusion.1, f32[2560]{0:T(1024)S(1)} %reduce.2), kind=kOutput, calls=%fused_computation.26 | convolution fusion | flops 1889566720 | bytes 16160512 | tf_op jit(solution)/shard_map/dot_general | solution.py:72
  295.6 8.5 %collective-permute-start = (bf16[128,512]{1,0:T(8,128)(2,1)S(1)}, bf16[128,512]{1,0:T(8,128)(2,1)S(1)}, u32[]{:S(2)}, u32[]{:S(2)}) collective-permute-start(bf16[128,512]{1,0:T(8,128)(2,1)S(1)} %slice.55), channel_id=1, source_target_pairs={{0,1},{1,2},{2,3},{3,4},{4,5},{5,6},{6,7},{7,8},{8,9},{9,10},{10,1... | collective-permute-start | bytes 393224 | tf_op jit(solution)/shard_map/ppermute | solution.py:16
  312.2 3.3 multiply_reduce_fusion.1
  317.5 4.6 gather_fusion
  322.0 4.5 select_multiply_fusion
  326.5 4.9 gather_fusion.1
  331.4 2.5 broadcast_select_fusion
  334.4 92.7 %all_to_all.15 = bf16[16,80,2880]{2,1,0:T(8,128)(2,1)S(1)} all-to-all(bf16[16,80,2880]{2,1,0:T(8,128)(2,1)S(1)} %bitcast.117), channel_id=1, replica_groups=mesh['section'=8,'expert'=16] {'expert'}, dimensions={0} | all-to-all | bytes 14745600 | tf_op jit(solution)/shard_map/all_to_all | solution.py:135
  427.1 15.5 %fusion.2 = f32[1280,1440]{0,1:T(8,128)} fusion(bf16[1280,2880]{1,0:T(8,128)(2,1)S(1)} %bitcast.119, bf16[1,1,2880,1440]{2,3,1,0:T(8,128)(2,1)} %param.21), kind=kOutput, calls=%fused_computation.7 | convolution fusion | flops 10616832000 | bytes 23040000 | tf_op jit(solution)/shard_map/dot_general | solution.py:137
  442.6 11.9 %convolution_convert_fusion = bf16[1280,2880]{0,1:T(8,128)(2,1)} fusion(bf16[1,1,720,2880]{3,2,1,0:T(8,128)(2,1)S(1)} %bitcast.133, f32[1280,1440]{0,1:T(8,128)} %fusion.2), kind=kOutput, calls=%fused_computation.6 | convolution fusion | flops 5319475200 | bytes 18892800 | tf_op jit(solution)/shard_map/dot_general | solution.py:139
  454.5 10.4 %copy.55 = bf16[1280,2880]{1,0:T(8,128)(2,1)} copy(bf16[1280,2880]{0,1:T(8,128)(2,1)} %convolution_convert_fusion) | data formatting | bytes 14745600 | tf_op jit(solution)/shard_map/convert_element_type | solution.py:140
  464.9 4.8 all-to-all-start.2
  470.1 91.4 %all-to-all-done.2 = bf16[16,80,2880]{2,1,0:T(8,128)(2,1)} async-done(((bf16[16,80,2880]{2,1,0:T(8,128)(2,1)}), bf16[16,80,2880]{2,1,0:T(8,128)(2,1)}, u32[]{:S(2)}, u32[]{:S(2)}) %all-to-all-start.2) | async-done | bytes 7372832 | tf_op jit(solution)/shard_map/all_to_all | solution.py:138
  561.5 9.5 %convert.3 = f32[8,2,80,2880]{3,2,1,0:T(8,128)} convert(bf16[8,2,80,2880]{3,2,1,0:T(8,128)(2,1)} %bitcast.37) | non-fusion elementwise | flops 3686400 | bytes 22118400 | tf_op jit(solution)/shard_map/reshape | solution.py:147
  571.1 7.8 %fusion.5 = bf16[8,1,80,2880]{3,2,0,1:T(8,128)(2,1)} fusion(f32[8,2,80,2880]{3,2,1,0:T(8,128)} %convert.3), kind=kLoop, calls=%fused_computation.11 | loop fusion | flops 3686400 | bytes 18432000 | tf_op jit(solution)/shard_map/convert_element_type | solution.py:150
  578.9 9.3 %gather_fusion.2 = bf16[512,2880]{1,0:T(8,128)(2,1)} fusion(bf16[640,2880]{1,0:T(8,128)(2,1)} %bitcast.115, s32[1024]{0:T(1024)S(1)} %pad_clamp_fusion), kind=kCustom, calls=%fused_computation.2 | custom fusion | bytes 5900288 | tf_op jit(solution)/shard_map/jit(_take)/gather | solution.py:153
  588.1 4.9 gather.24
  594.5 4.5 multiply_reduce_fusion
  602.1 12.1 %collective-permute-done.1 = bf16[128,2880]{0,1:T(8,128)(2,1)S(1)} collective-permute-done((bf16[128,2880]{0,1:T(8,128)(2,1)S(1)}, bf16[128,2880]{0,1:T(8,128)(2,1)S(1)}, u32[]{:S(2)}, u32[]{:S(2)}) %collective-permute-start.1) | collective-permute-done | bytes 737312 | tf_op jit(solution)/shard_map/ppermute | solution.py:21
  (100 shorter events, 22.6 us)
Async XLA Ops:
  6.6 8.2 %copy-start.8 = (s32[1,128,4]{1,2,0:T(4,128)S(1)}, s32[1,128,4]{1,2,0:T(4,128)}, u32[]{:S(2)}) copy-start(s32[1,128,4]{1,2,0:T(4,128)} %param.23) | copy-start | bytes 6148
  6.6 8.6 %copy-start.4 = (f32[1,2880]{1,0:T(1,128)S(1)}, f32[1,2880]{1,0:T(1,128)}, u32[]{:S(2)}) copy-start(f32[1,2880]{1,0:T(1,128)} %param.14) | copy-start | bytes 34564
  6.6 8.7 %copy-start.7 = (f32[1,2560]{1,0:T(1,128)S(1)}, f32[1,2560]{1,0:T(1,128)}, u32[]{:S(2)}) copy-start(f32[1,2560]{1,0:T(1,128)} %param.16) | copy-start | bytes 30724
  6.6 10.2 %copy-start.9 = (s32[1,8]{1,0:T(1,128)S(1)}, s32[1,8]{1,0:T(1,128)}, u32[]{:S(2)}) copy-start(s32[1,8]{1,0:T(1,128)} %param.25) | copy-start | bytes 100
  6.6 18.5 %copy-start.2 = (bf16[1,128,2880]{1,2,0:T(8,128)(2,1)S(1)}, bf16[1,128,2880]{1,2,0:T(8,128)(2,1)}, u32[]{:S(2)}) copy-start(bf16[1,128,2880]{1,2,0:T(8,128)(2,1)} %param.13) | copy-start | bytes 2211844
  6.6 268.0 %all-to-all-start = ((bf16[16,180,2560]{2,1,0:T(8,128)(2,1)}), bf16[16,180,2560]{2,1,0:T(8,128)(2,1)}, u32[]{:S(2)}, u32[]{:S(2)}) async-start(bf16[16,180,2560]{2,1,0:T(8,128)(2,1)} %stack.3), calls=%async_computation | async-start | bytes 30146560 | tf_op jit(solution)/shard_map/all_to_all | solution.py:63
  288.1 16.1 %copy-start.5 = (f32[1,2880]{1,0:T(1,128)S(1)}, f32[1,2880]{1,0:T(1,128)}, u32[]{:S(2)}) copy-start(f32[1,2880]{1,0:T(1,128)} %param.18) | copy-start | bytes 34564
  288.1 16.7 %copy-start.10 = (f32[1,32]{1,0:T(1,128)S(1)}, f32[1,32]{1,0:T(1,128)}, u32[]{:S(2)}) copy-start(f32[1,32]{1,0:T(1,128)} %param.19) | copy-start | bytes 388
  288.1 17.4 %copy-start.6 = (f32[1,2880]{1,0:T(1,128)S(1)}, f32[1,2880]{1,0:T(1,128)}, u32[]{:S(2)}) copy-start(f32[1,2880]{1,0:T(1,128)} %param.20) | copy-start | bytes 34564
  295.6 10.8 %collective-permute-start = (bf16[128,512]{1,0:T(8,128)(2,1)S(1)}, bf16[128,512]{1,0:T(8,128)(2,1)S(1)}, u32[]{:S(2)}, u32[]{:S(2)}) collective-permute-start(bf16[128,512]{1,0:T(8,128)(2,1)S(1)} %slice.55), channel_id=1, source_target_pairs={{0,1},{1,2},{2,3},{3,4},{4,5},{5,6},{6,7},{7,8},{8,9},{9,10},{10,1... | collective-permute-start | bytes 393224 | tf_op jit(solution)/shard_map/ppermute | solution.py:16
  307.6 2.5 slice-start
  308.7 2.5 slice-start.1
  308.7 3.5 slice-start.2
  315.5 1.2 copy-start
  334.4 108.2 %slice-start.3 = ((s8[4239360]{0:T(1024)(128)(4,1)}), s8[45056]{0:T(1024)(128)(4,1)S(1)}, s32[]{:S(2)}) async-start(s8[4239360]{0:T(1024)(128)(4,1)} %bitcast.132), calls=%async_computation.6 | async-start | bytes 90112
  427.1 15.5 %slice-start.4 = ((s8[4239360]{0:T(1024)(128)(4,1)}), s8[4194304]{0:T(1024)(128)(4,1)S(1)}, s32[]{:S(2)}) async-start(s8[4239360]{0:T(1024)(128)(4,1)} %bitcast.132), calls=%async_computation.7 | async-start | bytes 8388608
  464.9 5.0 copy-start.3
  464.9 96.6 %all-to-all-start.2 = ((bf16[16,80,2880]{2,1,0:T(8,128)(2,1)}), bf16[16,80,2880]{2,1,0:T(8,128)(2,1)}, u32[]{:S(2)}, u32[]{:S(2)}) async-start(bf16[16,80,2880]{2,1,0:T(8,128)(2,1)} %bitcast.116), calls=%async_computation.2 | async-start | bytes 15073280 | tf_op jit(solution)/shard_map/all_to_all | solution.py:138
  594.5 6.1 copy-start.1
  602.1 12.1 %collective-permute-start.1 = (bf16[128,2880]{0,1:T(8,128)(2,1)S(1)}, bf16[128,2880]{0,1:T(8,128)(2,1)S(1)}, u32[]{:S(2)}, u32[]{:S(2)}) collective-permute-start(bf16[128,2880]{0,1:T(8,128)(2,1)S(1)} %add_convert_fusion), channel_id=1, source_target_pairs={{0,16},{16,32},{32,48},{48,64},{64,80},{80,96},{96,112},{112,0},{1... | collective-permute-start | bytes 2211848 | tf_op jit(solution)/shard_map/ppermute | solution.py:21
